TPU v7x, 32 devices: a whole 2x2x4 slice. The times are simulated.
32 devices in a mesh: wide: 8 (over z, y), lev: 4 (over x, core).
Axes of the slice: x: 2, y: 2, z: 4, core: 2. Of those that a mesh axis runs over, the one named last changes fastest.
Arguments:
- state_field: float32 [12, 1472, 1472], P('lev', 'wide'), may hold values from -8 to 8
- to_modes: float32 [12, 12], replicated, may hold values from -4 to 4
- from_modes: float32 [12, 12], replicated, may hold values from -4 to 4, as said below
- mode_depth: float32 [12], replicated, may hold values from 0.1 to 2000
Outputs:
- updated_field: float32 [12, 1472, 1472], P('lev', 'wide')
Inputs may be any that keep to these rules, and one draw needn't show every extreme that they name: `from_modes`: the inverse of to_modes.
All inputs are finite; a program needn't handle non-finite values.
Results may differ from a plain program's by a relative error of at most 0.000094.
Values sent between devices are 32-bit elements; how exact they have to be, the bound alone decides.
No kernel may reach another device: no remote copies, remote signals or barrier semaphores. Data moves between devices by JAX's collectives and lax.ppermute only.
A program may use at most 64 MiB of HBM per device.

v0:
```python
import math
import jax
import jax.numpy as jnp
from jax import lax
from jax.sharding import PartitionSpec as P

I = 1472
E = 64
KT = 512
highest = lax.Precision.HIGHEST


def spread(block, axis, owner):
    block = jnp.where(lax.axis_index(axis) == owner, block, jnp.zeros_like(block))
    return lax.psum(block, axis)


def blend_weights(fraction):
    square = fraction * fraction
    cubed = square * fraction
    return (
        2.0 * cubed - 3.0 * square + 1.0,
        cubed - 2.0 * square + fraction,
        -2.0 * cubed + 3.0 * square,
        cubed - square,
    )


def hermite_mix(start_val, start_slope, end_val, end_slope, weights):
    return (
        weights[0] * end_val
        + weights[1] * end_slope
        + weights[2] * start_val
        + weights[3] * start_slope
    )


def extend_cols(sub_block, extra):
    fraction = (jnp.arange(extra, dtype=jnp.float32) + 1.0) / (extra + 1.0)
    weights = blend_weights(fraction)
    end_val = sub_block[..., -1:]
    end_slope = sub_block[..., -1:] - sub_block[..., -2:-1]
    start_val = sub_block[..., :1]
    start_slope = sub_block[..., 1:2] - sub_block[..., :1]
    added = hermite_mix(start_val, start_slope, end_val, end_slope, weights)
    return jnp.concatenate([sub_block, added], axis=-1)


def laplace(waves, length):
    sines = jnp.sin(math.pi / length * waves.astype(jnp.float32))
    return 4.0 * sines * sines


def cas_table(positions, waves, length):
    product = positions[:, None] * waves[None, :] % length
    phase_angle = 2.0 * math.pi / length * product.astype(jnp.float32)
    return jnp.cos(phase_angle) + jnp.sin(phase_angle)


def wave_numbers(amount, length, bound):
    indices = jnp.arange(amount, dtype=jnp.int32)
    waves = jnp.where(indices < bound, indices, length - 2 * bound + 1 + indices)
    live_mask = indices < 2 * bound - 1
    waves = jnp.where(live_mask, waves, 0)
    magnitude = jnp.minimum(waves, length - waves)
    return (waves, live_mask.astype(jnp.float32), magnitude)


def shards(state_field, to_modes, from_modes, mode_depth):
    wide_count = lax.axis_size("wide")
    wide_index = lax.axis_index("wide")
    lev_index = lax.axis_index("lev")
    levels, row_count, col_count = state_field.shape
    length = I + E
    ext_count = E // wide_count
    row_total = row_count + ext_count
    head_strip = spread(state_field[:, :2], "wide", 0)
    tail_strip = spread(state_field[:, row_count - 2 :], "wide", wide_count - 1)
    ext_slot = (wide_count - wide_index) % wide_count
    row_ids = ext_slot * ext_count + jnp.arange(ext_count, dtype=jnp.int32)
    fraction = (row_ids.astype(jnp.float32) + 1.0) / (E + 1.0)
    weights = tuple((weight[:, None] for weight in blend_weights(fraction)))
    end_val = tail_strip[:, 1:2]
    end_slope = tail_strip[:, 1:2] - tail_strip[:, 0:1]
    start_val = head_strip[:, 0:1]
    start_slope = head_strip[:, 1:2] - head_strip[:, 0:1]
    ext_block = hermite_mix(start_val, start_slope, end_val, end_slope, weights)
    stacked = jnp.concatenate([state_field, ext_block], axis=1)
    widened = extend_cols(stacked, E)
    spec_count = 2 * KT
    waves, live_mask, magnitude = wave_numbers(spec_count, length, KT)
    lap_all = laplace(waves, length)
    positions = jnp.arange(length, dtype=jnp.int32)
    forward_x = cas_table(positions, waves, length) * live_mask[None, :]
    row_owner = positions // row_total
    local_row = positions % row_total
    ext_owner = (wide_count - row_owner) % wide_count
    row_pos = jnp.where(
        local_row < row_count,
        row_owner * row_count + local_row,
        I + ext_owner * ext_count + local_row - row_count,
    )
    forward_y = cas_table(row_pos, waves, length) * live_mask[None, :]
    inverse_y = forward_y.T / length
    inverse_x = forward_x[:I].T / length
    col_span = spec_count // wide_count
    col_start = wide_index * col_span
    spec_x = jnp.einsum("irn,nc->irc", widened, forward_x, precision=highest)
    spectrum = jnp.einsum(
        "irc,rk->ick",
        lax.all_to_all(spec_x, "wide", split_axis=2, concat_axis=1, tiled=True),
        forward_y,
        precision=highest,
    )
    lev_start = lev_index * levels
    sub_block = lax.dynamic_slice(to_modes, (0, lev_start), (lax.axis_size("lev") * levels, levels))
    mode_values = lax.psum_scatter(
        jnp.einsum("ml,lck->mck", sub_block, spectrum, precision=highest),
        "lev",
        scatter_dimension=0,
        tiled=True,
    )
    lap_cols = lax.dynamic_slice_in_dim(lap_all, col_start, col_span)
    mag_cols = lax.dynamic_slice_in_dim(magnitude, col_start, col_span)
    live_cols = lax.dynamic_slice_in_dim(live_mask, col_start, col_span)
    inside = (
        mag_cols[:, None] * mag_cols[:, None] + magnitude[None, :] * magnitude[None, :] < KT * KT
    )
    keep_mask = live_cols[:, None] * live_mask[None, :] * inside.astype(jnp.float32)
    keep_mask, lap_sum = (keep_mask, lap_cols[:, None] + lap_all[None, :])
    mode_rates = lax.dynamic_slice_in_dim(mode_depth, lev_start, levels)
    solved = mode_values * keep_mask / (1.0 + mode_rates[:, None, None] * lap_sum)
    shard_piece = lax.all_gather(solved, "lev", axis=0, tiled=True)
    sub_block = lax.dynamic_slice(from_modes, (lev_start, 0), (levels, shard_piece.shape[0]))
    mixed_levels = jnp.einsum("lm,mck->lck", sub_block, shard_piece, precision=highest)
    rows_back = jnp.einsum("ick,kr->icr", mixed_levels, inverse_y, precision=highest)
    return jnp.einsum(
        "icr,cn->irn",
        lax.all_to_all(rows_back, "wide", split_axis=2, concat_axis=1, tiled=True)[
            :, :, :row_count
        ],
        inverse_x,
        precision=highest,
    )


def solution(mesh):
    placed = (P("lev", "wide", None), P(), P(), P())
    return jax.shard_map(
        shards, mesh=mesh, in_specs=placed, out_specs=P("lev", "wide", None), check_vma=False
    )
```

profile of v0, /device:TPU:0, one launch (start us, length us, event | category | flops | bytes accessed | tf_op | source)
XLA Modules:
  0.0 513.1 jit_solution(13678874333688489325)
XLA Ops:
  6.5 0.0 copy-start
  6.5 0.0 copy-start.4
  6.5 0.0 all-reduce.3.cloned.1.call-start
  6.5 1.8 slice_select_fusion.1
  8.3 0.0 all-reduce.3.cloned.1.call-update
  8.5 74.6 %all-reduce.3.cloned.1.call-done = (f32[3,2,1472]{2,1,0:T(2,128)}, f32[3,2,1472]{2,1,0:T(2,128)}) async-done(((f32[3,2,1472]{2,1,0:T(2,128)}, f32[3,2,1472]{2,1,0:T(2,128)}), (f32[3,2,1472]{2,1,0:T(2,128)}, f32[3,2,1472]{2,1,0:T(2,128)})) %all-reduce.3.cloned.1.call-update) | async-done | bytes 70672 | tf_op jit(solution)/shard_map/psum | solution.py:15
  83.1 0.9 fusion.107
  84.1 0.1 multiply_add_fusion.1
  84.2 2.0 fusion.66
  86.2 0.4 multiply_add_fusion
  86.6 0.0 copy-done.4
  86.6 0.4 fusion.124
  87.0 38.5 %fusion.12 = f32[3,192,1024]{2,1,0:T(8,128)S(1)} fusion(f32[1024]{0:T(1024)S(1)} %fusion.85, s32[1024]{0:T(1024)S(1)} %fusion.86, f32[3,192,1536]{2,1,0:T(8,128)S(1)} %fusion.124), kind=kOutput, calls=%fused_computation.15 | convolution fusion | flops 10888937472 | bytes 5906432 | tf_op jit(solution)/shard_map/irn,nc->irc/dot_general | solution.py:108
  125.5 3.2 copy.32
  128.7 4.8 all-to-all-start
  133.5 0.0 reduce-scatter.2.cloned.1.call-start
  133.5 91.4 %all-to-all-done = f32[3,192,1024]{1,0,2:T(4,128)} async-done(((f32[3,192,1024]{1,0,2:T(4,128)}), f32[3,192,1024]{1,0,2:T(4,128)}, u32[]{:S(2)}, u32[]{:S(2)}) %all-to-all-start) | async-done | bytes 2359328 | tf_op jit(solution)/shard_map/all_to_all | solution.py:111
  224.9 3.4 copy.45
  228.3 41.6 %fusion.10 = f32[3,128,1024]{2,1,0:T(8,128)S(1)} fusion(f32[3,1536,128]{2,1,0:T(8,128)S(1)} %bitcast.57, s32[1536]{0:T(1024)S(1)} %fusion.78, f32[1024]{0:T(1024)S(1)} %fusion.85, s32[1024]{0:T(1024)S(1)} %fusion.86), kind=kOutput, calls=%fused_computation.13 | convolution fusion | flops 7265058816 | bytes 3946496 | tf_op jit(solution)/shard_map/irc,rk->ick/dot_general | solution.py:109
  270.0 0.0 copy-done
  270.0 7.3 %fusion.59 = f32[12,128,1024]{2,0,1:T(8,128)S(1)} fusion(f32[3,128,1024]{2,1,0:T(8,128)S(1)} %fusion.10, f32[12,12]{1,0:T(8,128)S(1)} %copy-done, s32[]{:T(128)S(6)} %select_n.144), kind=kOutput, calls=%fused_computation.63 | convolution fusion | flops 56623104 | bytes 7864900 | tf_op jit(solution)/shard_map/ml,lck->mck/dot_general | solution.py:118
  277.3 6.3 %copy.37 = f32[12,128,1024]{2,1,0:T(8,128)} copy(f32[12,128,1024]{2,0,1:T(8,128)S(1)} %fusion.59) | data formatting | bytes 12582912 | tf_op jit(solution)/shard_map/ml,lck->mck/dot_general | solution.py:118
  283.6 0.0 copy-start.5
  283.6 0.0 reduce-scatter.2.cloned.1.call-update
  283.6 0.0 all-gather.2.cloned.1.call-start
  283.7 0.1 dynamic_slice.21
  283.8 0.1 dynamic_slice.23
  283.9 0.4 copy-done.5
  284.3 0.1 dynamic_slice.22
  284.3 0.1 dynamic-slice_multiply_fusion
  284.4 0.1 broadcast_add_fusion
  284.5 0.2 multiply_select_fusion
  284.7 56.9 %reduce-scatter.2.cloned.1.call-done = f32[3,128,1024]{2,1,0:T(8,128)} async-done(((f32[12,128,1024]{2,1,0:T(8,128)}), f32[3,128,1024]{2,1,0:T(8,128)}) %reduce-scatter.2.cloned.1.call-update) | async-done | bytes 1572880 | tf_op jit(solution)/shard_map/reduce_scatter | solution.py:117
  341.7 2.9 add_divide_fusion
  344.6 0.0 all-gather.2.cloned.1.call-update
  344.7 27.9 %fusion.122 = f32[1024,1536,1]{1,0,2:T(8,128)} fusion(f32[1024]{0:T(1024)S(1)} %fusion.85, s32[1024]{0:T(1024)S(1)} %fusion.86, s32[1536]{0:T(1024)S(1)} %fusion.78), kind=kLoop, calls=%fused_computation.12.clone.1 | loop fusion | flops 18874368 | bytes 6305792 | tf_op jit(solution)/shard_map/ick,kr->icr/dot_general | solution.py:136
  372.5 18.7 %all-gather.2.cloned.1.call-done = f32[12,128,1024]{2,1,0:T(8,128)} async-done(((f32[3,128,1024]{2,1,0:T(8,128)}), f32[12,128,1024]{2,1,0:T(8,128)}) %all-gather.2.cloned.1.call-update) | async-done | bytes 6291472 | tf_op jit(solution)/shard_map/all_gather | solution.py:133
  391.2 0.0 copy-start.2
  391.2 11.3 %fusion = f32[3,128,1024]{2,0,1:T(4,128)S(1)} fusion(f32[12,128,1024]{2,1,0:T(8,128)} %all-gather.2.cloned.1.call-done, f32[12,12]{1,0:T(8,128)} %param.6, s32[]{:T(128)S(6)} %select_n.144), kind=kOutput, calls=%fused_computation.3 | convolution fusion | flops 56623104 | bytes 7866372 | tf_op jit(solution)/shard_map/lm,mck->lck/dot_general | solution.py:135
  402.5 0.0 copy-done.2
  402.5 8.6 %fusion.8 = f32[3,128,1536]{2,1,0:T(8,128)S(1)} fusion(f32[3,128,1024]{2,0,1:T(4,128)S(1)} %fusion, f32[1024,1536,1]{1,0,2:T(8,128)S(1)} %copy-done.2), kind=kOutput, calls=%fused_computation.11 | convolution fusion | flops 7247757312 | bytes 10223616 | tf_op jit(solution)/shard_map/ick,kr->icr/dot_general | solution.py:136
  411.1 2.7 copy.40
  413.9 5.8 %all-to-all-start.1 = ((f32[3,128,1536]{1,0,2:T(4,128)}), f32[3,128,1536]{1,0,2:T(4,128)S(1)}, u32[]{:S(2)}, u32[]{:S(2)}) async-start(f32[3,128,1536]{1,0,2:T(4,128)} %copy.40), calls=%async_computation.2 | async-start | bytes 6291456 | tf_op jit(solution)/shard_map/all_to_all | solution.py:139
  419.6 27.2 %add_multiply_fusion = f32[1536,1024]{1,0:T(8,128)} fusion(f32[1024]{0:T(1024)S(1)} %fusion.85, s32[1024]{0:T(1024)S(1)} %fusion.86), kind=kLoop, calls=%fused_computation.32 | loop fusion | flops 17301504 | bytes 6299648 | tf_op jit(solution)/shard_map/mul | solution.py:94
  446.8 43.9 %all-to-all-done.1 = f32[3,128,1536]{1,0,2:T(4,128)S(1)} async-done(((f32[3,128,1536]{1,0,2:T(4,128)}), f32[3,128,1536]{1,0,2:T(4,128)S(1)}, u32[]{:S(2)}, u32[]{:S(2)}) %all-to-all-start.1) | async-done | bytes 2359328 | tf_op jit(solution)/shard_map/all_to_all | solution.py:139
  490.7 0.0 copy-start.3
  490.7 0.2 copy.41
  490.9 0.0 copy-start.1
  490.9 0.3 copy.64
  491.2 2.3 copy-done.3
  493.5 12.7 %fusion.37 = f32[3,184,1472]{2,1,0:T(8,128)} fusion(f32[1536,1024]{1,0:T(8,128)S(1)} %copy-done.3, f32[3,1024,192]{1,2,0:T(8,128)S(1)} %bitcast.56), kind=kOutput, calls=%fused_computation.41 | convolution fusion | flops 9986048000 | bytes 11540480 | tf_op jit(solution)/shard_map/icr,cn->irn/dot_general | solution.py:137
  506.2 0.0 copy-done.1
  (14 shorter events, 0.2 us)
Async XLA Ops:
  6.5 263.4 %copy-start = (f32[12,12]{1,0:T(8,128)S(1)}, f32[12,12]{1,0:T(8,128)}, u32[]{:S(2)}) copy-start(f32[12,12]{1,0:T(8,128)} %param.5) | copy-start | bytes 1732
  6.5 80.1 %copy-start.4 = (f32[3,184,1472]{2,1,0:T(8,128)S(1)}, f32[3,184,1472]{2,1,0:T(8,128)}, u32[]{:S(2)}) copy-start(f32[3,184,1472]{2,1,0:T(8,128)} %param.4) | copy-start | bytes 9750532
  6.5 76.5 %all-reduce.3.cloned.1.call-start = ((), (), s32[]{:S(2)}) async-start(), calls=%async_computation.5 | async-start | bytes 147456 | tf_op jit(solution)/shard_map/psum | solution.py:15
  128.7 96.2 %all-to-all-start = ((f32[3,192,1024]{1,0,2:T(4,128)}), f32[3,192,1024]{1,0,2:T(4,128)}, u32[]{:S(2)}, u32[]{:S(2)}) async-start(f32[3,192,1024]{1,0,2:T(4,128)} %copy.32), calls=%async_computation | async-start | bytes 8388608 | tf_op jit(solution)/shard_map/all_to_all | solution.py:111
  133.5 208.2 %reduce-scatter.2.cloned.1.call-start = ((), (), s32[]{:S(2)}) async-start(), calls=%async_computation.3 | async-start | bytes 7864320 | tf_op jit(solution)/shard_map/reduce_scatter | solution.py:117
  283.6 0.7 copy-start.5
  283.6 107.5 %all-gather.2.cloned.1.call-start = ((), (), s32[]{:S(2)}) async-start(), calls=%async_computation.4 | async-start | bytes 7864320 | tf_op jit(solution)/shard_map/all_gather | solution.py:133
  391.2 11.4 %copy-start.2 = (f32[1024,1536,1]{1,0,2:T(8,128)S(1)}, f32[1024,1536,1]{1,0,2:T(8,128)}, u32[]{:S(2)}) copy-start(f32[1024,1536,1]{1,0,2:T(8,128)} %fusion.122) | copy-start | bytes 18874372
  413.9 76.8 %all-to-all-start.1 = ((f32[3,128,1536]{1,0,2:T(4,128)}), f32[3,128,1536]{1,0,2:T(4,128)S(1)}, u32[]{:S(2)}, u32[]{:S(2)}) async-start(f32[3,128,1536]{1,0,2:T(4,128)} %copy.40), calls=%async_computation.2 | async-start | bytes 6291456 | tf_op jit(solution)/shard_map/all_to_all | solution.py:139
  490.7 2.8 copy-start.3
  490.9 15.3 %copy-start.1 = (f32[12,12]{1,0:T(8,128)S(1)}, f32[12,12]{1,0:T(8,128)}, u32[]{:S(2)}) copy-start(f32[12,12]{1,0:T(8,128)} %param.5) | copy-start | bytes 1732
Sparse Core Ops, SparseCore 0:
  10.8 72.1 all-reduce.2
  283.8 57.8 reduce-scatter.1
  344.8 46.3 all-gather.1
where the time goes:
time: 522 us; the launch traced here: 513 us
  waiting for transfers between devices  286 us (55%)
  matrix products  120 us (23%)
  other arithmetic  64.1 us (12%)
  local copies, waits for them, and re-layouts  19 us (4%)
  between operations  13.7 us (3%)
  starting transfers between devices  10.6 us (2%)
    all_to_all x1, waiting for transfers between devices, shards(): lax.all_to_all(spec_x, 'wide', split_axis=2, concat_axis=1, tiled=True)  91.4 us
    psum x1, waiting for transfers between devices, spread(): return lax.psum(block, axis)  74.6 us
    reduce_scatter x1, waiting for transfers between devices, shards(): lax.psum_scatter(jnp.einsum('ml,lck->mck', sub_block, spectrum, precision...  56.9 us
    all_to_all x1, waiting for transfers between devices, shards(): lax.all_to_all(rows_back, 'wide', split_axis=2, concat_axis=1, tiled=True)  43.9 us
    dot_general x1, matrix products, shards(): jnp.einsum('irc,rk->ick', lax.all_to_all(spec_x, 'wide', split_axis=2, co...  41.6 us
    dot_general x1, matrix products, shards(): spec_x = jnp.einsum('irn,nc->irc', widened, forward_x, precision=highest)  38.5 us
    dot_general x1, other arithmetic, shards(): jnp.einsum('ick,kr->icr', mixed_levels, inverse_y, precision=highest)  27.9 us
    mul x1, other arithmetic, shards(): forward_x = cas_table(positions, waves, length) * live_mask[None, :]  27.2 us
  transfers between devices with their start and end apart: 5, of which 5 were waited for; matrix products, arithmetic and copies ran while one was open for 11% of the time, Pallas kernels for 0%

commit v1 on v0

--- a/solution.py
+++ b/solution.py
@@ -10,9 +10,15 @@
 highest = lax.Precision.HIGHEST
 
 
+def add_all(x, axis):
+    parts = lax.all_gather(x, axis, axis=0, tiled=False)
+    acc = parts.sum(axis=0)
+    return acc
+
+
 def spread(block, axis, owner):
     block = jnp.where(lax.axis_index(axis) == owner, block, jnp.zeros_like(block))
-    return lax.psum(block, axis)
+    return add_all(block, axis)
 
 
 def blend_weights(fraction):

time: 522 us -> 500 us (0.958); the launches traced: 513 us -> 497 us
  waiting for transfers between devices: 286 us -> 200 us
  blocking collectives: 0 us -> 67.4 us
    psum x1 -> x0, waiting for transfers between devices: 74.6 us -> none  [spread(): return lax.psum(block, axis)]
    all_gather x0 -> x2, blocking collectives: none -> 67.4 us  [add_all(): parts = lax.all_gather(x, axis, axis=0, tiled=False)]
    all_to_all x1, waiting for transfers between devices: 91.4 us -> 80.6 us  [shards(): lax.all_to_all(spec_x, 'wide', split_axis=2, concat_axis=1, tiled=True)]
  transfers between devices with their start and end apart: 5 -> 4, of which waited for: 5 -> 4; matrix products, arithmetic and copies ran while one was open for 11% -> 11% of each run, Pallas kernels for 0% -> 0%
where the time goes in v1:
time: 500 us; the launch traced here: 497 us
  waiting for transfers between devices  200 us (40%)
  matrix products  120 us (24%)
  blocking collectives  67.4 us (13%)
  other arithmetic  64.7 us (13%)
  local copies, waits for them, and re-layouts  19.2 us (4%)
  between operations  13.9 us (3%)
  starting transfers between devices  11.5 us (2%)
    all_to_all x1, waiting for transfers between devices, shards(): lax.all_to_all(spec_x, 'wide', split_axis=2, concat_axis=1, tiled=True)  80.6 us
    all_gather x2, blocking collectives, add_all(): parts = lax.all_gather(x, axis, axis=0, tiled=False)  67.4 us
    reduce_scatter x1, waiting for transfers between devices, shards(): lax.psum_scatter(jnp.einsum('ml,lck->mck', sub_block, spectrum, precision...  56.7 us
    all_to_all x1, waiting for transfers between devices, shards(): lax.all_to_all(rows_back, 'wide', split_axis=2, concat_axis=1, tiled=True)  43.9 us
    dot_general x1, matrix products, shards(): jnp.einsum('irc,rk->ick', lax.all_to_all(spec_x, 'wide', split_axis=2, co...  41.6 us
    dot_general x1, matrix products, shards(): spec_x = jnp.einsum('irn,nc->irc', widened, forward_x, precision=highest)  38.7 us
    dot_general x1, other arithmetic, shards(): jnp.einsum('ick,kr->icr', mixed_levels, inverse_y, precision=highest)  27.9 us
    mul x1, other arithmetic, shards(): forward_x = cas_table(positions, waves, length) * live_mask[None, :]  27.2 us
  transfers between devices with their start and end apart: 4, of which 4 were waited for; matrix products, arithmetic and copies ran while one was open for 11% of the time, Pallas kernels for 0%

profile of v1, /device:TPU:0, one launch (start us, length us, event | category | flops | bytes accessed | tf_op | source)
XLA Modules:
  0.0 496.9 jit_solution(11500988414860721161)
XLA Ops:
  6.5 0.0 copy-start
  6.5 0.0 copy-start.4
  6.6 1.2 slice_select_fusion.1
  7.8 34.6 %all-gather.1 = f32[24,2,1472]{2,1,0:T(2,128)} all-gather(f32[3,2,1472]{2,1,0:T(2,128)S(1)} %get-tuple-element.10), channel_id=3, replica_groups=mesh['wide'=8,'lev'=4] {'wide'}, dimensions={0}, use_global_device_ids=true | all-gather | bytes 317952 | tf_op jit(solution)/shard_map/all_gather | solution.py:14
  42.4 1.1 reduce_sum.19
  43.5 32.8 %all-gather = f32[24,2,1472]{2,1,0:T(2,128)} all-gather(f32[3,2,1472]{2,1,0:T(2,128)S(1)} %get-tuple-element.9), channel_id=2, replica_groups=mesh['wide'=8,'lev'=4] {'wide'}, dimensions={0}, use_global_device_ids=true | all-gather | bytes 317952 | tf_op jit(solution)/shard_map/all_gather | solution.py:14
  76.3 1.1 reduce_sum.18
  77.5 0.1 multiply_add_fusion.1
  77.6 2.0 fusion.66
  79.6 0.4 multiply_add_fusion
  80.0 0.0 copy-done.4
  80.0 0.4 fusion.124
  80.4 38.7 %fusion.12 = f32[3,192,1024]{2,1,0:T(8,128)S(1)} fusion(f32[1024]{0:T(1024)S(1)} %fusion.85, s32[1024]{0:T(1024)S(1)} %fusion.86, f32[3,192,1536]{2,1,0:T(8,128)S(1)} %fusion.124), kind=kOutput, calls=%fused_computation.15 | convolution fusion | flops 10888937472 | bytes 5906432 | tf_op jit(solution)/shard_map/irn,nc->irc/dot_general | solution.py:114
  119.1 3.2 copy.32
  122.2 5.7 %all-to-all-start = ((f32[3,192,1024]{1,0,2:T(4,128)}), f32[3,192,1024]{1,0,2:T(4,128)}, u32[]{:S(2)}, u32[]{:S(2)}) async-start(f32[3,192,1024]{1,0,2:T(4,128)} %copy.32), calls=%async_computation | async-start | bytes 8388608 | tf_op jit(solution)/shard_map/all_to_all | solution.py:117
  127.9 0.0 reduce-scatter.2.cloned.1.call-start
  128.0 80.6 %all-to-all-done = f32[3,192,1024]{1,0,2:T(4,128)} async-done(((f32[3,192,1024]{1,0,2:T(4,128)}), f32[3,192,1024]{1,0,2:T(4,128)}, u32[]{:S(2)}, u32[]{:S(2)}) %all-to-all-start) | async-done | bytes 2359328 | tf_op jit(solution)/shard_map/all_to_all | solution.py:117
  208.6 3.6 copy.45
  212.2 41.6 %fusion.10 = f32[3,128,1024]{2,1,0:T(8,128)S(1)} fusion(f32[3,1536,128]{2,1,0:T(8,128)S(1)} %bitcast.55, s32[1536]{0:T(1024)S(1)} %fusion.78, f32[1024]{0:T(1024)S(1)} %fusion.85, s32[1024]{0:T(1024)S(1)} %fusion.86), kind=kOutput, calls=%fused_computation.13 | convolution fusion | flops 7265058816 | bytes 3946496 | tf_op jit(solution)/shard_map/irc,rk->ick/dot_general | solution.py:115
  253.8 0.0 copy-done
  253.8 7.3 %fusion.59 = f32[12,128,1024]{2,0,1:T(8,128)S(1)} fusion(f32[3,128,1024]{2,1,0:T(8,128)S(1)} %fusion.10, f32[12,12]{1,0:T(8,128)S(1)} %copy-done, s32[]{:T(128)S(6)} %select_n.144), kind=kOutput, calls=%fused_computation.63 | convolution fusion | flops 56623104 | bytes 7864900 | tf_op jit(solution)/shard_map/ml,lck->mck/dot_general | solution.py:124
  261.2 6.3 %copy.37 = f32[12,128,1024]{2,1,0:T(8,128)} copy(f32[12,128,1024]{2,0,1:T(8,128)S(1)} %fusion.59) | data formatting | bytes 12582912 | tf_op jit(solution)/shard_map/ml,lck->mck/dot_general | solution.py:124
  267.4 0.0 copy-start.5
  267.4 0.0 reduce-scatter.2.cloned.1.call-update
  267.5 0.0 all-gather.4.cloned.1.call-start
  267.5 0.1 dynamic_slice.21
  267.6 0.1 dynamic_slice.23
  267.7 0.4 copy-done.5
  268.1 0.1 dynamic_slice.22
  268.2 0.1 dynamic-slice_multiply_fusion
  268.3 0.1 broadcast_add_fusion
  268.4 0.2 multiply_select_fusion
  268.6 56.7 %reduce-scatter.2.cloned.1.call-done = f32[3,128,1024]{2,1,0:T(8,128)} async-done(((f32[12,128,1024]{2,1,0:T(8,128)}), f32[3,128,1024]{2,1,0:T(8,128)}) %reduce-scatter.2.cloned.1.call-update) | async-done | bytes 1572880 | tf_op jit(solution)/shard_map/reduce_scatter | solution.py:123
  325.3 2.9 add_divide_fusion
  328.3 0.0 all-gather.4.cloned.1.call-update
  328.3 27.9 %fusion.122 = f32[1024,1536,1]{1,0,2:T(8,128)} fusion(f32[1024]{0:T(1024)S(1)} %fusion.85, s32[1024]{0:T(1024)S(1)} %fusion.86, s32[1536]{0:T(1024)S(1)} %fusion.78), kind=kLoop, calls=%fused_computation.12.clone.1 | loop fusion | flops 18874368 | bytes 6305792 | tf_op jit(solution)/shard_map/ick,kr->icr/dot_general | solution.py:142
  356.1 18.7 %all-gather.4.cloned.1.call-done = f32[12,128,1024]{2,1,0:T(8,128)} async-done(((f32[3,128,1024]{2,1,0:T(8,128)}), f32[12,128,1024]{2,1,0:T(8,128)}) %all-gather.4.cloned.1.call-update) | async-done | bytes 6291472 | tf_op jit(solution)/shard_map/all_gather | solution.py:139
  374.8 0.0 copy-start.2
  374.8 11.3 %fusion = f32[3,128,1024]{2,0,1:T(4,128)S(1)} fusion(f32[12,128,1024]{2,1,0:T(8,128)} %all-gather.4.cloned.1.call-done, f32[12,12]{1,0:T(8,128)} %param.6, s32[]{:T(128)S(6)} %select_n.144), kind=kOutput, calls=%fused_computation.3 | convolution fusion | flops 56623104 | bytes 7866372 | tf_op jit(solution)/shard_map/lm,mck->lck/dot_general | solution.py:141
  386.1 0.0 copy-done.2
  386.2 8.6 %fusion.8 = f32[3,128,1536]{2,1,0:T(8,128)S(1)} fusion(f32[3,128,1024]{2,0,1:T(4,128)S(1)} %fusion, f32[1024,1536,1]{1,0,2:T(8,128)S(1)} %copy-done.2), kind=kOutput, calls=%fused_computation.11 | convolution fusion | flops 7247757312 | bytes 10223616 | tf_op jit(solution)/shard_map/ick,kr->icr/dot_general | solution.py:142
  394.8 2.7 copy.40
  397.5 5.8 %all-to-all-start.1 = ((f32[3,128,1536]{1,0,2:T(4,128)}), f32[3,128,1536]{1,0,2:T(4,128)S(1)}, u32[]{:S(2)}, u32[]{:S(2)}) async-start(f32[3,128,1536]{1,0,2:T(4,128)} %copy.40), calls=%async_computation.2 | async-start | bytes 6291456 | tf_op jit(solution)/shard_map/all_to_all | solution.py:145
  403.3 27.2 %add_multiply_fusion = f32[1536,1024]{1,0:T(8,128)} fusion(f32[1024]{0:T(1024)S(1)} %fusion.85, s32[1024]{0:T(1024)S(1)} %fusion.86), kind=kLoop, calls=%fused_computation.32 | loop fusion | flops 17301504 | bytes 6299648 | tf_op jit(solution)/shard_map/mul | solution.py:100
  430.4 43.9 %all-to-all-done.1 = f32[3,128,1536]{1,0,2:T(4,128)S(1)} async-done(((f32[3,128,1536]{1,0,2:T(4,128)}), f32[3,128,1536]{1,0,2:T(4,128)S(1)}, u32[]{:S(2)}, u32[]{:S(2)}) %all-to-all-start.1) | async-done | bytes 2359328 | tf_op jit(solution)/shard_map/all_to_all | solution.py:145
  474.3 0.0 copy-start.3
  474.3 0.2 copy.41
  474.5 0.0 copy-start.1
  474.5 0.3 copy.64
  474.8 2.3 copy-done.3
  477.1 12.7 %fusion.37 = f32[3,184,1472]{2,1,0:T(8,128)} fusion(f32[1536,1024]{1,0:T(8,128)S(1)} %copy-done.3, f32[3,1024,192]{1,2,0:T(8,128)S(1)} %bitcast.54), kind=kOutput, calls=%fused_computation.41 | convolution fusion | flops 9986048000 | bytes 11540480 | tf_op jit(solution)/shard_map/icr,cn->irn/dot_general | solution.py:143
  489.8 0.0 copy-done.1
  (14 shorter events, 0.2 us)
Async XLA Ops:
  6.5 247.3 %copy-start = (f32[12,12]{1,0:T(8,128)S(1)}, f32[12,12]{1,0:T(8,128)}, u32[]{:S(2)}) copy-start(f32[12,12]{1,0:T(8,128)} %param.5) | copy-start | bytes 1732
  6.5 73.5 %copy-start.4 = (f32[3,184,1472]{2,1,0:T(8,128)S(1)}, f32[3,184,1472]{2,1,0:T(8,128)}, u32[]{:S(2)}) copy-start(f32[3,184,1472]{2,1,0:T(8,128)} %param.4) | copy-start | bytes 9750532
  122.2 86.3 %all-to-all-start = ((f32[3,192,1024]{1,0,2:T(4,128)}), f32[3,192,1024]{1,0,2:T(4,128)}, u32[]{:S(2)}, u32[]{:S(2)}) async-start(f32[3,192,1024]{1,0,2:T(4,128)} %copy.32), calls=%async_computation | async-start | bytes 8388608 | tf_op jit(solution)/shard_map/all_to_all | solution.py:117
  127.9 197.4 %reduce-scatter.2.cloned.1.call-start = ((), (), s32[]{:S(2)}) async-start(), calls=%async_computation.3 | async-start | bytes 7864320 | tf_op jit(solution)/shard_map/reduce_scatter | solution.py:123
  267.4 0.7 copy-start.5
  267.5 107.3 %all-gather.4.cloned.1.call-start = ((), (), s32[]{:S(2)}) async-start(), calls=%async_computation.4 | async-start | bytes 7864320 | tf_op jit(solution)/shard_map/all_gather | solution.py:139
  374.8 11.4 %copy-start.2 = (f32[1024,1536,1]{1,0,2:T(8,128)S(1)}, f32[1024,1536,1]{1,0,2:T(8,128)}, u32[]{:S(2)}) copy-start(f32[1024,1536,1]{1,0,2:T(8,128)} %fusion.122) | copy-start | bytes 18874372
  397.5 76.8 %all-to-all-start.1 = ((f32[3,128,1536]{1,0,2:T(4,128)}), f32[3,128,1536]{1,0,2:T(4,128)S(1)}, u32[]{:S(2)}, u32[]{:S(2)}) async-start(f32[3,128,1536]{1,0,2:T(4,128)} %copy.40), calls=%async_computation.2 | async-start | bytes 6291456 | tf_op jit(solution)/shard_map/all_to_all | solution.py:145
  474.3 2.8 copy-start.3
  474.5 15.3 %copy-start.1 = (f32[12,12]{1,0:T(8,128)S(1)}, f32[12,12]{1,0:T(8,128)}, u32[]{:S(2)}) copy-start(f32[12,12]{1,0:T(8,128)} %param.5) | copy-start | bytes 1732
Sparse Core Ops, SparseCore 0:
  267.6 57.6 reduce-scatter.1
  328.4 46.3 all-gather.3
